TPU v7x, 128 devices: a whole 4x4x4 slice. The times are simulated.
128 devices in a mesh: tm: 32 (over x, y, core), chan: 4 (over z).
Axes of the slice: x: 4, y: 4, z: 4, core: 2. Of those that a mesh axis runs over, the one named last changes fastest.
Arguments:
- samples: float32 [64, 1048576], P('chan', 'tm'), may hold values from -6 to 6
- start_basis: float32 [512, 128], replicated, may hold values from -6 to 6
Outputs:
- factor: float32 [1024, 1024], P(('tm', 'chan'))
- states: float32 [128, 1048576], P(None, ('tm', 'chan'))
All inputs are finite; a program needn't handle non-finite values.
Results may differ from a plain program's by a relative error of at most 0.0003.
Values sent between devices are 32-bit elements; how exact they have to be, the bound alone decides.
No kernel may reach another device: no remote copies, remote signals or barrier semaphores. Data moves between devices by JAX's collectives and lax.ppermute only.
A program may use at most 256 MiB of HBM per device.

v0:
```python
import jax
import jax.numpy as jnp
from jax import lax
from jax.sharding import PartitionSpec as P

BR = 16
NSTEPS = 6


def from_behind(array, axis, by):
    size = lax.axis_size(axis)
    pairs = [(i, i + by) for i in range(size) if 0 <= i + by < size]
    return lax.ppermute(array, axis, pairs)


def upper_factor(gram):
    return jnp.linalg.cholesky(gram).T


def outer_gram(left, right):
    return lax.dot_general(
        left,
        right,
        (((1,), (1,)), ((), ())),
        precision=lax.Precision.HIGHEST,
        preferred_element_type=jnp.float32,
    )


def per_device(samples, start_basis):
    local = lax.all_to_all(samples, "chan", split_axis=1, concat_axis=0, tiled=True)
    count = local.shape[1]
    following = from_behind(local[:, : BR - 1], ("tm", "chan"), -1)
    extended = jnp.concatenate([local, following], 1)
    hankel = jnp.concatenate([extended[:, k : k + count] for k in range(BR)], 0)
    order = hankel.shape[0]
    half = order // 2
    total = count * lax.axis_size("tm") * lax.axis_size("chan")
    weight = 1.0 / (1.0 + jnp.mean(local * local, 0))
    gram = outer_gram(hankel * weight[None, :], hankel) * (1.0 / total)
    gram = lax.psum(gram, ("tm", "chan"))
    factor = upper_factor(gram)
    lead = jnp.dot(
        factor[half:, half:].T,
        start_basis,
        precision=lax.Precision.HIGHEST,
        preferred_element_type=jnp.float32,
    )
    basis = lead / jnp.sqrt(jnp.sum(lead * lead))
    for step in range(NSTEPS):
        inner = jnp.dot(
            basis.T, basis, precision=lax.Precision.HIGHEST, preferred_element_type=jnp.float32
        )
        basis = 1.5 * basis - 0.5 * jnp.dot(
            basis, inner, precision=lax.Precision.HIGHEST, preferred_element_type=jnp.float32
        )
    states = jnp.dot(
        basis.T, hankel[half:], precision=lax.Precision.HIGHEST, preferred_element_type=jnp.float32
    )
    share = order // (lax.axis_size("tm") * lax.axis_size("chan"))
    position = lax.axis_index(("tm", "chan"))
    mine = lax.dynamic_slice_in_dim(factor, position * share, share, 0)
    return (mine, states)


def solution(mesh):
    placed = (P("chan", "tm"), P())
    return jax.shard_map(
        per_device,
        mesh=mesh,
        in_specs=placed,
        out_specs=(P(("tm", "chan"), None), P(None, ("tm", "chan"))),
        check_vma=False,
    )
```

profile of v0, /device:TPU:1, one launch (start us, length us, event | category | flops | bytes accessed | tf_op | source)
XLA Modules:
  0.0 616.3 jit_solution(9280351724594159771)
XLA Ops:
  7.2 1.8 copy.55
  9.0 31.1 %all_to_all.19 = f32[16,4,8192]{2,0,1:T(8,128)S(1)} all-to-all(f32[16,4,8192]{2,0,1:T(8,128)S(1)} %bitcast.102), channel_id=1, replica_groups=mesh['tm'=32,'chan'=4] {'chan'}, dimensions={1} | all-to-all | bytes 4194304 | tf_op jit(solution)/shard_map/all_to_all | solution.py:31
  40.1 4.5 collective-permute-start
  44.9 0.8 collective-permute-done
  48.7 2.1 fusion.53
  50.8 2.5 fusion.65
  53.2 1.9 fusion.11
  55.2 2.0 fusion.13
  57.1 2.0 fusion.15
  59.1 1.9 fusion.17
  61.1 2.0 fusion.19
  63.0 1.9 fusion.21
  65.0 2.0 fusion.64
  66.9 1.9 fusion.62
  68.9 1.9 fusion.60
  70.8 2.0 fusion.58
  72.8 2.0 fusion.56
  74.8 1.9 fusion.54
  76.7 2.0 fusion.66
  78.6 2.2 fusion.30
  80.8 5.7 copy-done.2
  86.5 118.2 %fusion.4 = f32[1024,1024]{0,1:T(8,128)} fusion(f32[1024,8192]{1,0:T(8,128)} %get-tuple-element.11, f32[8192]{0:T(1024)S(1)} %add_divide_fusion), kind=kOutput, calls=%fused_computation.21 | convolution fusion | flops 103088652288 | bytes 37781504 | tf_op jit(solution)/shard_map/dot_general | solution.py:21
  204.7 157.1 %all-reduce.3.cloned.1.call-done = f32[1024,1024]{0,1:T(8,128)} async-done(((f32[1024,1024]{0,1:T(8,128)}), f32[1024,1024]{0,1:T(8,128)}) %all-reduce.3.cloned.1.call-update) | async-done | bytes 4194320 | tf_op jit(solution)/shard_map/psum | solution.py:41
  361.8 5.3 copy.37
  367.2 4.4 fusion.3
  371.6 2.0 copy-done.3
  373.6 11.7 %cholesky.223 = f32[128,128]{1,0:T(8,128)S(1)} custom-call(f32[128,128]{1,0:T(8,128)S(1)} %cholesky.580), custom_call_target="Cholesky" | custom-call | tf_op jit(solution)/shard_map/jit(cholesky)/cholesky | solution.py:17
  385.4 9.8 %custom-call.59 = f32[1,128,128]{1,2,0:T(8,128)S(1)} custom-call(f32[1,128,128]{2,1,0:T(8,128)S(1)} %get-tuple-element.37), custom_call_target="InvertDiagBlocksLowerTriangular" | custom-call | tf_op jit(solution)/shard_map/jit(cholesky)/cholesky | solution.py:17
  395.2 1.6 fusion.51
  397.0 1.9 slice_subtract_fusion
  399.0 2.5 cholesky.255
  401.4 12.1 %cholesky.244 = f32[128,128]{1,0:T(8,128)S(1)} custom-call(f32[128,128]{1,0:T(8,128)S(1)} %cholesky.584), custom_call_target="Cholesky" | custom-call | tf_op jit(solution)/shard_map/jit(cholesky)/cholesky | solution.py:17
  413.5 0.9 constant_dynamic-update-slice_fusion.7
  415.1 9.8 %custom-call.60 = f32[1,128,128]{1,2,0:T(8,128)S(1)} custom-call(f32[1,128,128]{2,1,0:T(8,128)S(1)} %get-tuple-element.34), custom_call_target="InvertDiagBlocksLowerTriangular" | custom-call | tf_op jit(solution)/shard_map/jit(cholesky)/cholesky | solution.py:17
  424.9 1.3 convolution_dynamic-update-slice_fusion
  426.1 2.1 slice_subtract_fusion.1
  428.3 11.7 %cholesky.468 = f32[128,128]{1,0:T(8,128)S(1)} custom-call(f32[128,128]{1,0:T(8,128)S(1)} %cholesky.589), custom_call_target="Cholesky" | custom-call | tf_op jit(solution)/shard_map/jit(cholesky)/cholesky | solution.py:17
  441.3 9.8 %custom-call.61 = f32[1,128,128]{1,2,0:T(8,128)S(1)} custom-call(f32[1,128,128]{2,1,0:T(8,128)S(1)} %get-tuple-element.31), custom_call_target="InvertDiagBlocksLowerTriangular" | custom-call | tf_op jit(solution)/shard_map/jit(cholesky)/cholesky | solution.py:17
  451.1 1.2 convolution_dynamic-update-slice_fusion.1
  452.3 2.3 slice_subtract_fusion.2
  454.6 11.9 %cholesky.487 = f32[128,128]{1,0:T(8,128)S(1)} custom-call(f32[128,128]{1,0:T(8,128)S(1)} %cholesky.594), custom_call_target="Cholesky" | custom-call | tf_op jit(solution)/shard_map/jit(cholesky)/cholesky | solution.py:17
  467.8 9.8 %custom-call.62 = f32[1,128,128]{1,2,0:T(8,128)S(1)} custom-call(f32[1,128,128]{2,1,0:T(8,128)S(1)} %get-tuple-element.28), custom_call_target="InvertDiagBlocksLowerTriangular" | custom-call | tf_op jit(solution)/shard_map/jit(cholesky)/cholesky | solution.py:17
  477.6 1.1 convolution_dynamic-update-slice_fusion.2
  478.7 2.3 slice_subtract_fusion.3
  481.1 11.7 %cholesky.506 = f32[128,128]{1,0:T(8,128)S(1)} custom-call(f32[128,128]{1,0:T(8,128)S(1)} %cholesky.599), custom_call_target="Cholesky" | custom-call | tf_op jit(solution)/shard_map/jit(cholesky)/cholesky | solution.py:17
  493.4 0.7 compare_reduce_fusion.3
  494.1 10.0 %custom-call.63 = f32[1,128,128]{1,2,0:T(8,128)S(1)} custom-call(f32[1,128,128]{2,1,0:T(8,128)S(1)} %get-tuple-element.25), custom_call_target="InvertDiagBlocksLowerTriangular" | custom-call | tf_op jit(solution)/shard_map/jit(cholesky)/cholesky | solution.py:17
  504.1 1.0 convolution_dynamic-update-slice_fusion.3
  505.2 2.3 slice_subtract_fusion.4
  507.4 11.7 %cholesky.526 = f32[128,128]{1,0:T(8,128)S(1)} custom-call(f32[128,128]{1,0:T(8,128)S(1)} %cholesky.604), custom_call_target="Cholesky" | custom-call | tf_op jit(solution)/shard_map/jit(cholesky)/cholesky | solution.py:17
  520.4 9.8 %custom-call.64 = f32[1,128,128]{1,2,0:T(8,128)S(1)} custom-call(f32[1,128,128]{2,1,0:T(8,128)S(1)} %get-tuple-element.22), custom_call_target="InvertDiagBlocksLowerTriangular" | custom-call | tf_op jit(solution)/shard_map/jit(cholesky)/cholesky | solution.py:17
  530.3 0.9 convolution_dynamic-update-slice_fusion.4
  531.2 2.0 slice_subtract_fusion.5
  533.3 12.1 %cholesky.546 = f32[128,128]{1,0:T(8,128)S(1)} custom-call(f32[128,128]{1,0:T(8,128)S(1)} %cholesky.609), custom_call_target="Cholesky" | custom-call | tf_op jit(solution)/shard_map/jit(cholesky)/cholesky | solution.py:17
  546.6 9.8 %custom-call.65 = f32[1,128,128]{1,2,0:T(8,128)S(1)} custom-call(f32[1,128,128]{2,1,0:T(8,128)S(1)} %get-tuple-element.19), custom_call_target="InvertDiagBlocksLowerTriangular" | custom-call | tf_op jit(solution)/shard_map/jit(cholesky)/cholesky | solution.py:17
  556.4 0.9 convolution_dynamic-update-slice_fusion.5
  557.3 1.8 slice_subtract_fusion.6
  559.1 11.7 %cholesky.564 = f32[128,128]{1,0:T(8,128)S(1)} custom-call(f32[128,128]{1,0:T(8,128)S(1)} %slice_subtract_fusion.6), custom_call_target="Cholesky" | custom-call | tf_op jit(solution)/shard_map/jit(cholesky)/cholesky | solution.py:17
  577.8 2.8 fusion.130
  581.2 2.5 select_select_fusion
  583.7 1.6 multiply_reduce_fusion
  592.0 1.2 dynamic-slice_bitcast_fusion
  593.3 0.8 copy.45
  594.0 15.2 %fusion.103 = f32[128,8192]{1,0:T(8,128)} fusion(f32[512,128]{1,0:T(8,128)S(1)} %fusion.31, f32[512,8192]{1,0:T(8,128)} %copy-done.2), kind=kOutput, calls=%fused_computation.168 | convolution fusion | flops 6442450944 | bytes 21233664 | tf_op jit(solution)/shard_map/dot_general | solution.py:57
  (50 shorter events, 18.6 us)
Async XLA Ops:
  7.2 576.6 %copy-start = (f32[512,128]{1,0:T(8,128)S(1)}, f32[512,128]{1,0:T(8,128)}, u32[]{:S(2)}) copy-start(f32[512,128]{1,0:T(8,128)} %param.3) | copy-start | bytes 786436
  7.2 354.6 %all-reduce.3.cloned.1.call-start = ((), (), s32[]{:S(2)}) async-start(), calls=%async_computation.1 | async-start | bytes 8388608 | tf_op jit(solution)/shard_map/psum | solution.py:41
  40.1 5.5 collective-permute-start
  80.8 5.7 copy-start.2
  371.6 2.0 copy-start.3
  577.8 3.5 copy-start.1
Sparse Core Ops, SparseCore 0:
  204.8 156.9 all-reduce.2
where the time goes:
time: 626 us; the launch traced here: 616 us
  other arithmetic  218 us (35%)
  matrix products  164 us (26%)
  waiting for transfers between devices  158 us (25%)
  blocking collectives  31.1 us (5%)
  local copies, waits for them, and re-layouts  21.1 us (3%)
  between operations  20.2 us (3%)
    another operation x30, other arithmetic, upper_factor(): return jnp.linalg.cholesky(gram).T  173 us
    psum x1, waiting for transfers between devices, per_device(): gram = lax.psum(gram, ('tm', 'chan'))  157 us
    dot_general x1, matrix products, outer_gram(): lax.dot_general(left, right, (((1,), (1,)), ((), ())), precision=lax.Prec...  118 us
    unnamed x20, other arithmetic  33 us
    all_to_all x1, blocking collectives, per_device(): lax.all_to_all(samples, 'chan', split_axis=1, concat_axis=0, tiled=True)  31.1 us
    another operation x14, matrix products, upper_factor(): return jnp.linalg.cholesky(gram).T  22.8 us
    dot_general x1, matrix products, per_device(): jnp.dot(basis.T, hankel[half:], precision=lax.Precision.HIGHEST, preferre...  15.2 us
  transfers between devices with their start and end apart: 2, of which 2 were waited for; matrix products, arithmetic and copies ran while one was open for 0% of the time, Pallas kernels for 0%

commit v1 on v0

--- a/solution.py
+++ b/solution.py
@@ -38,7 +38,7 @@
     total = count * lax.axis_size("tm") * lax.axis_size("chan")
     weight = 1.0 / (1.0 + jnp.mean(local * local, 0))
     gram = outer_gram(hankel * weight[None, :], hankel) * (1.0 / total)
-    gram = lax.psum(gram, ("tm", "chan"))
+    gram = lax.psum(lax.psum(gram, "chan"), "tm")
     factor = upper_factor(gram)
     lead = jnp.dot(
         factor[half:, half:].T,

time: 626 us -> 679 us (1.085)
  waiting for transfers between devices: 158 us -> 212 us
    psum x1 -> x2, waiting for transfers between devices: 157 us -> 211 us  [per_device(): gram = lax.psum(lax.psum(gram, 'chan'), 'tm')]
  transfers between devices with their start and end apart: 2 -> 3, of which waited for: 2 -> 3; matrix products, arithmetic and copies ran while one was open for 0% -> 0% of each run, Pallas kernels for 0% -> 0%
where the time goes in v1:
time: 679 us; the launch traced here: 670 us
  other arithmetic  218 us (32%)
  waiting for transfers between devices  212 us (31%)
  matrix products  164 us (24%)
  blocking collectives  31.1 us (5%)
  local copies, waits for them, and re-layouts  21.1 us (3%)
  between operations  20.3 us (3%)
    psum x2, waiting for transfers between devices, per_device(): gram = lax.psum(lax.psum(gram, 'chan'), 'tm')  211 us
    another operation x30, other arithmetic, upper_factor(): return jnp.linalg.cholesky(gram).T  173 us
    dot_general x1, matrix products, outer_gram(): lax.dot_general(left, right, (((1,), (1,)), ((), ())), precision=lax.Prec...  118 us
    unnamed x20, other arithmetic  33 us
    all_to_all x1, blocking collectives, per_device(): lax.all_to_all(samples, 'chan', split_axis=1, concat_axis=0, tiled=True)  31.1 us
    another operation x14, matrix products, upper_factor(): return jnp.linalg.cholesky(gram).T  22.8 us
    dot_general x1, matrix products, per_device(): jnp.dot(basis.T, hankel[half:], precision=lax.Precision.HIGHEST, preferre...  15.2 us
  transfers between devices with their start and end apart: 3, of which 3 were waited for; matrix products, arithmetic and copies ran while one was open for 0% of the time, Pallas kernels for 0%

profile of v1, /device:TPU:1, one launch (start us, length us, event | category | flops | bytes accessed | tf_op | source)
XLA Modules:
  0.0 670.0 jit_solution(18112390807650637938)
XLA Ops:
  7.2 1.8 copy.55
  9.0 31.1 %all_to_all.19 = f32[16,4,8192]{2,0,1:T(8,128)S(1)} all-to-all(f32[16,4,8192]{2,0,1:T(8,128)S(1)} %bitcast.102), channel_id=1, replica_groups=mesh['tm'=32,'chan'=4] {'chan'}, dimensions={1} | all-to-all | bytes 4194304 | tf_op jit(solution)/shard_map/all_to_all | solution.py:31
  40.1 4.5 collective-permute-start
  44.9 0.8 collective-permute-done
  48.7 2.1 fusion.47
  50.8 2.5 fusion.59
  53.2 1.9 fusion.11
  55.2 2.0 fusion.13
  57.1 2.0 fusion.15
  59.1 1.9 fusion.17
  61.1 2.0 fusion.19
  63.0 1.9 fusion.21
  65.0 2.0 fusion.58
  66.9 1.9 fusion.56
  68.9 1.9 fusion.54
  70.8 2.0 fusion.52
  72.8 2.0 fusion.50
  74.8 1.9 fusion.48
  76.7 2.0 fusion.60
  78.6 2.2 fusion.30
  80.8 5.7 copy-done.2
  86.5 118.2 %fusion.4 = f32[1024,1024]{0,1:T(8,128)} fusion(f32[1024,8192]{1,0:T(8,128)} %get-tuple-element.11, f32[8192]{0:T(1024)S(1)} %add_divide_fusion), kind=kOutput, calls=%fused_computation.21 | convolution fusion | flops 103088652288 | bytes 37781504 | tf_op jit(solution)/shard_map/dot_general | solution.py:21
  204.7 95.9 %all-reduce.4.cloned.1.call-done = f32[1024,1024]{0,1:T(8,128)} async-done(((f32[1024,1024]{0,1:T(8,128)}), f32[1024,1024]{0,1:T(8,128)}) %all-reduce.4.cloned.1.call-update) | async-done | bytes 4194320 | tf_op jit(solution)/shard_map/psum | solution.py:41
  300.7 114.9 %all-reduce.6.cloned.1.call-done = f32[1024,1024]{0,1:T(8,128)} async-done(((f32[1024,1024]{0,1:T(8,128)}), f32[1024,1024]{0,1:T(8,128)}) %all-reduce.6.cloned.1.call-update) | async-done | bytes 4194320 | tf_op jit(solution)/shard_map/psum | solution.py:41
  415.6 5.3 copy.37
  420.9 4.4 fusion.3
  425.3 2.0 copy-done.3
  427.4 11.7 %cholesky.223 = f32[128,128]{1,0:T(8,128)S(1)} custom-call(f32[128,128]{1,0:T(8,128)S(1)} %cholesky.580), custom_call_target="Cholesky" | custom-call | tf_op jit(solution)/shard_map/jit(cholesky)/cholesky | solution.py:17
  439.1 9.8 %custom-call.59 = f32[1,128,128]{1,2,0:T(8,128)S(1)} custom-call(f32[1,128,128]{2,1,0:T(8,128)S(1)} %get-tuple-element.37), custom_call_target="InvertDiagBlocksLowerTriangular" | custom-call | tf_op jit(solution)/shard_map/jit(cholesky)/cholesky | solution.py:17
  448.9 1.6 fusion.45
  450.8 1.9 convolution_subtract_fusion
  452.7 2.5 cholesky.255
  455.2 12.1 %cholesky.244 = f32[128,128]{1,0:T(8,128)S(1)} custom-call(f32[128,128]{1,0:T(8,128)S(1)} %cholesky.584), custom_call_target="Cholesky" | custom-call | tf_op jit(solution)/shard_map/jit(cholesky)/cholesky | solution.py:17
  467.3 0.9 constant_dynamic-update-slice_fusion.7
  468.8 9.8 %custom-call.60 = f32[1,128,128]{1,2,0:T(8,128)S(1)} custom-call(f32[1,128,128]{2,1,0:T(8,128)S(1)} %get-tuple-element.34), custom_call_target="InvertDiagBlocksLowerTriangular" | custom-call | tf_op jit(solution)/shard_map/jit(cholesky)/cholesky | solution.py:17
  478.6 1.3 convolution_dynamic-update-slice_fusion
  479.9 2.1 convolution_subtract_fusion.1
  482.0 11.7 %cholesky.468 = f32[128,128]{1,0:T(8,128)S(1)} custom-call(f32[128,128]{1,0:T(8,128)S(1)} %cholesky.589), custom_call_target="Cholesky" | custom-call | tf_op jit(solution)/shard_map/jit(cholesky)/cholesky | solution.py:17
  495.0 9.8 %custom-call.61 = f32[1,128,128]{1,2,0:T(8,128)S(1)} custom-call(f32[1,128,128]{2,1,0:T(8,128)S(1)} %get-tuple-element.31), custom_call_target="InvertDiagBlocksLowerTriangular" | custom-call | tf_op jit(solution)/shard_map/jit(cholesky)/cholesky | solution.py:17
  504.8 1.2 convolution_dynamic-update-slice_fusion.1
  506.0 2.3 convolution_subtract_fusion.2
  508.4 11.9 %cholesky.487 = f32[128,128]{1,0:T(8,128)S(1)} custom-call(f32[128,128]{1,0:T(8,128)S(1)} %cholesky.594), custom_call_target="Cholesky" | custom-call | tf_op jit(solution)/shard_map/jit(cholesky)/cholesky | solution.py:17
  521.5 9.8 %custom-call.62 = f32[1,128,128]{1,2,0:T(8,128)S(1)} custom-call(f32[1,128,128]{2,1,0:T(8,128)S(1)} %get-tuple-element.28), custom_call_target="InvertDiagBlocksLowerTriangular" | custom-call | tf_op jit(solution)/shard_map/jit(cholesky)/cholesky | solution.py:17
  531.4 1.1 convolution_dynamic-update-slice_fusion.2
  532.4 2.3 convolution_subtract_fusion.3
  534.8 11.7 %cholesky.506 = f32[128,128]{1,0:T(8,128)S(1)} custom-call(f32[128,128]{1,0:T(8,128)S(1)} %cholesky.599), custom_call_target="Cholesky" | custom-call | tf_op jit(solution)/shard_map/jit(cholesky)/cholesky | solution.py:17
  547.9 10.0 %custom-call.63 = f32[1,128,128]{1,2,0:T(8,128)S(1)} custom-call(f32[1,128,128]{2,1,0:T(8,128)S(1)} %get-tuple-element.25), custom_call_target="InvertDiagBlocksLowerTriangular" | custom-call | tf_op jit(solution)/shard_map/jit(cholesky)/cholesky | solution.py:17
  557.9 1.0 convolution_dynamic-update-slice_fusion.3
  558.9 2.3 convolution_subtract_fusion.4
  561.2 11.7 %cholesky.526 = f32[128,128]{1,0:T(8,128)S(1)} custom-call(f32[128,128]{1,0:T(8,128)S(1)} %cholesky.604), custom_call_target="Cholesky" | custom-call | tf_op jit(solution)/shard_map/jit(cholesky)/cholesky | solution.py:17
  574.2 9.8 %custom-call.64 = f32[1,128,128]{1,2,0:T(8,128)S(1)} custom-call(f32[1,128,128]{2,1,0:T(8,128)S(1)} %get-tuple-element.22), custom_call_target="InvertDiagBlocksLowerTriangular" | custom-call | tf_op jit(solution)/shard_map/jit(cholesky)/cholesky | solution.py:17
  584.0 0.9 convolution_dynamic-update-slice_fusion.4
  584.9 2.0 convolution_subtract_fusion.5
  587.0 12.1 %cholesky.546 = f32[128,128]{1,0:T(8,128)S(1)} custom-call(f32[128,128]{1,0:T(8,128)S(1)} %cholesky.609), custom_call_target="Cholesky" | custom-call | tf_op jit(solution)/shard_map/jit(cholesky)/cholesky | solution.py:17
  600.4 9.8 %custom-call.65 = f32[1,128,128]{1,2,0:T(8,128)S(1)} custom-call(f32[1,128,128]{2,1,0:T(8,128)S(1)} %get-tuple-element.19), custom_call_target="InvertDiagBlocksLowerTriangular" | custom-call | tf_op jit(solution)/shard_map/jit(cholesky)/cholesky | solution.py:17
  610.2 0.9 convolution_dynamic-update-slice_fusion.5
  611.0 1.8 convolution_subtract_fusion.6
  612.8 11.7 %cholesky.564 = f32[128,128]{1,0:T(8,128)S(1)} custom-call(f32[128,128]{1,0:T(8,128)S(1)} %convolution_subtract_fusion.6), custom_call_target="Cholesky" | custom-call | tf_op jit(solution)/shard_map/jit(cholesky)/cholesky | solution.py:17
  631.5 2.8 fusion.113
  635.0 2.5 select_select_fusion
  637.5 1.6 multiply_reduce_fusion
  645.7 1.2 dynamic-slice_bitcast_fusion
  647.0 0.8 copy.45
  647.8 15.2 %fusion.86 = f32[128,8192]{1,0:T(8,128)} fusion(f32[512,128]{1,0:T(8,128)S(1)} %fusion.31, f32[512,8192]{1,0:T(8,128)} %copy-done.2), kind=kOutput, calls=%fused_computation.161 | convolution fusion | flops 6442450944 | bytes 21233664 | tf_op jit(solution)/shard_map/dot_general | solution.py:57
  (53 shorter events, 19.4 us)
Async XLA Ops:
  7.2 630.3 %copy-start = (f32[512,128]{1,0:T(8,128)S(1)}, f32[512,128]{1,0:T(8,128)}, u32[]{:S(2)}) copy-start(f32[512,128]{1,0:T(8,128)} %param.3) | copy-start | bytes 786436
  7.2 293.5 %all-reduce.4.cloned.1.call-start = ((), (), s32[]{:S(2)}) async-start(), calls=%async_computation.1 | async-start | bytes 8388608 | tf_op jit(solution)/shard_map/psum | solution.py:41
  40.1 5.5 collective-permute-start
  80.8 5.7 copy-start.2
  204.7 210.9 %all-reduce.6.cloned.1.call-start = ((), (), s32[]{:S(2)}) async-start(), calls=%async_computation.2 | async-start | bytes 8388608 | tf_op jit(solution)/shard_map/psum | solution.py:41
  425.3 2.0 copy-start.3
  631.5 3.5 copy-start.1
Sparse Core Ops, SparseCore 0:
  204.8 95.8 all-reduce.3
  304.3 111.1 all-reduce.5
